TPU v7x, 512 devices: a whole 4x8x8 slice. The times are simulated.
512 devices in a mesh: dp: 128 (over y, z, core), mp: 4 (over x).
Axes of the slice: x: 4, y: 8, z: 8, core: 2. Of those that a mesh axis runs over, the one named last changes fastest.
Arguments:
- frames: bfloat16 [32768, 1024], P('dp'), may hold values from -24 to 24
- proj_in: bfloat16 [1024, 2, 1024], P(None, None, 'mp'), may hold values from -0.1875 to 0.1875
- depthwise: float32 [31, 1024], P(None, 'mp'), may hold values from -1 to 1
- bn_gain: float32 [1024], P('mp'), may hold values from 0.5 to 1.5
- bn_shift: float32 [1024], P('mp'), may hold values from -3 to 3
- proj_out: bfloat16 [1024, 1024], P(None, 'mp'), may hold values from -0.1875 to 0.1875
- grad_out: bfloat16 [32768, 1024], P('dp'), may hold values from -24 to 24
- counts: int32 [128], replicated, may hold values from 1 to 2, as said below
- lengths: int32 [128, 2], P('dp'), may hold values from 1 to 255, as said below
Outputs:
- frame_grad: bfloat16 [32768, 1024], P('dp', 'mp')
- in_grad: float32 [1024, 2, 1024], P('dp', None, 'mp')
- out_grad: float32 [1024, 1024], P('dp', 'mp')
- depth_grad: float32 [31, 1024], P(None, 'mp')
- gain_grad: float32 [1024], P('mp')
- shift_grad: float32 [1024], P('mp')
Inputs may be any that keep to these rules, and one draw needn't show every extreme that they name: `counts`: some device holds 2 live blocks. lengths[d] sums to 128 * counts[d]; on some device with 2 live blocks one utterance holds all frames but one for each other utterance.
All inputs are finite; a program needn't handle non-finite values.
Results may differ from a plain program's by a relative error of at most 0.0095.
Values may be sent and summed in bfloat16 or wider, within the bound.
No kernel may reach another device: no remote copies, remote signals or barrier semaphores. Data moves between devices by JAX's collectives and lax.ppermute only.
A program may use at most 64 MiB of HBM per device.

v0:
```python
import jax
import jax.numpy as jnp
from jax import lax
from jax.sharding import Mesh, PartitionSpec as P

BLOCK = 128
DP = ("y", "z", "core")


def time_shift(values, offset, fill_value):
    if offset > 0:
        pad_part = jnp.full((offset,) + values.shape[1:], fill_value, values.dtype)
        return jnp.concatenate([values[offset:], pad_part], axis=0)
    if offset < 0:
        pad_part = jnp.full((-offset,) + values.shape[1:], fill_value, values.dtype)
        return jnp.concatenate([pad_part, values[:offset]], axis=0)
    return values


def tap_term(glu_float, owner_id, live_col, offset):
    same_utt = (time_shift(owner_id, offset, -1) == owner_id).astype(jnp.float32)[
        :, None
    ] * live_col
    return time_shift(glu_float, offset, 0.0) * same_utt


def small_sum(x):
    x = lax.psum(x, "core")
    peers = lax.axis_size("y") * lax.axis_size("z")
    every = jnp.broadcast_to(x[None], (peers,) + x.shape)
    return jnp.sum(lax.all_to_all(every, ("y", "z"), 0, 0), axis=0)


def scatter_sum(partial):
    peers = lax.axis_size("y") * lax.axis_size("z")
    rows = partial.shape[0] // (2 * peers)
    parts = partial.reshape(peers, 2, rows, partial.shape[1])
    core = lax.axis_index("core")
    keep = lax.dynamic_index_in_dim(parts, core, 1, keepdims=False)
    send = lax.dynamic_index_in_dim(parts, 1 - core, 1, keepdims=False).astype(jnp.bfloat16)
    got = lax.ppermute(send, "core", [(0, 1), (1, 0)])
    both = (keep + got.astype(jnp.float32)).astype(jnp.bfloat16)
    every = lax.all_to_all(both, ("y", "z"), 0, 0)
    return jnp.sum(every.astype(jnp.float32), axis=0)


def shards(frames, proj_in, depthwise, bn_gain, bn_shift, proj_out, grad_out, counts, lengths):
    frames_dev = frames.shape[0]
    model_width = frames.shape[1]
    channels = proj_in.shape[2]
    tap_count = depthwise.shape[0]
    radius = tap_count // 2
    rows_dev = model_width // lax.axis_size(DP)
    groups = lax.axis_size("mp")
    position = jnp.arange(frames_dev, dtype=jnp.int32)
    utt_ends = jnp.cumsum(lengths[0])
    owner_id = jnp.sum((position[:, None] >= utt_ends[None, :]).astype(jnp.int32), axis=1)
    my_count = counts[lax.axis_index(DP)]
    live_col = (position < my_count * BLOCK).astype(jnp.float32)[:, None]
    frame_total = (jnp.sum(counts) * BLOCK).astype(jnp.float32)
    proj_flat = proj_in.reshape(model_width, 2 * channels)
    pre_act = jnp.dot(frames, proj_flat, preferred_element_type=jnp.float32)
    value_half = pre_act[:, :channels]
    gate_sig = jax.nn.sigmoid(pre_act[:, channels:])
    glu_out = (value_half * gate_sig * live_col).astype(jnp.bfloat16)
    glu_float = lax.optimization_barrier(glu_out).astype(jnp.float32)
    conv_out = jnp.zeros((frames_dev, channels), jnp.float32)
    for tap_index in range(tap_count):
        conv_out = conv_out + depthwise[tap_index] * tap_term(
            glu_float, owner_id, live_col, tap_index - radius
        )
    sum_val, sum_sq = small_sum(
        jnp.stack([jnp.sum(conv_out, axis=0), jnp.sum(conv_out * conv_out, axis=0)])
    )
    mean_val = sum_val / frame_total
    square_mean = sum_sq / frame_total
    inv_std = lax.rsqrt(square_mean - mean_val * mean_val + 1e-05)
    normed = (conv_out - mean_val) * inv_std
    scaled = normed * bn_gain + bn_shift
    sig_scaled = jax.nn.sigmoid(scaled)
    hidden = (scaled * sig_scaled * live_col).astype(jnp.bfloat16)
    grad_hidden = jnp.dot(grad_out, proj_out, preferred_element_type=jnp.float32) * live_col
    grad_scaled = grad_hidden * sig_scaled * (1.0 + scaled * (1.0 - sig_scaled))
    local_shift = jnp.sum(grad_scaled, axis=0)
    local_gain = jnp.sum(grad_scaled * normed, axis=0)
    shift_grad, gain_grad = small_sum(jnp.stack([local_shift, local_gain]))
    grad_conv = (
        live_col
        * bn_gain
        * inv_std
        * (grad_scaled - shift_grad / frame_total - normed * gain_grad / frame_total)
    )
    depth_rows = []
    for tap_index in range(tap_count):
        depth_rows.append(
            jnp.sum(grad_conv * tap_term(glu_float, owner_id, live_col, tap_index - radius), axis=0)
        )
    depth_grad = lax.psum(lax.psum(lax.psum(jnp.stack(depth_rows), "core"), "y"), "z")
    grad_glu = jnp.zeros((frames_dev, channels), jnp.float32)
    for tap_index in range(tap_count):
        offset = tap_index - radius
        back_same = (time_shift(owner_id, -offset, -1) == owner_id).astype(jnp.float32)[
            :, None
        ] * live_col
        grad_glu = grad_glu + depthwise[tap_index] * time_shift(grad_conv, -offset, 0.0) * back_same
    grad_value = grad_glu * gate_sig
    grad_gate = grad_glu * value_half * gate_sig * (1.0 - gate_sig)
    grad_flat = jnp.concatenate([grad_value, grad_gate], axis=1).astype(jnp.bfloat16)
    frame_term = lax.dot_general(
        proj_flat, grad_flat, (((1,), (1,)), ((), ())), preferred_element_type=jnp.float32
    ).T.astype(jnp.bfloat16)
    frame_parts = frame_term.reshape(frames_dev, groups, model_width // groups)
    frame_parts = lax.all_to_all(jnp.swapaxes(frame_parts, 0, 1), "mp", 0, 0)
    frame_grad = jnp.sum(frame_parts.astype(jnp.float32), axis=0).astype(jnp.bfloat16)
    summed = scatter_sum(
        jnp.concatenate(
            [
                lax.dot_general(
                    frames, grad_flat, (((0,), (0,)), ((), ())), preferred_element_type=jnp.float32
                ),
                lax.dot_general(
                    grad_out, hidden, (((0,), (0,)), ((), ())), preferred_element_type=jnp.float32
                ),
            ],
            axis=1,
        )
    )
    in_flat = summed[:, : 2 * channels]
    out_grad = summed[:, 2 * channels :]
    in_grad = in_flat.reshape(rows_dev, 2, channels)
    return (frame_grad, in_grad, out_grad, depth_grad, gain_grad, shift_grad)


def solution(mesh):
    grid = Mesh(mesh.devices.reshape(8, 8, 2, 4), ("y", "z", "core", "mp"))
    placed = (
        P(DP, None),
        P(None, None, "mp"),
        P(None, "mp"),
        P("mp"),
        P("mp"),
        P(None, "mp"),
        P(DP, None),
        P(),
        P(DP, None),
    )
    return jax.shard_map(
        shards,
        mesh=grid,
        in_specs=placed,
        out_specs=(P(DP, "mp"), P(DP, None, "mp"), P(DP, "mp"), P(None, "mp"), P("mp"), P("mp")),
        check_vma=False,
    )
```

profile of v0, /device:TPU:2, one launch (start us, length us, event | category | flops | bytes accessed | tf_op | source)
XLA Modules:
  0.0 197.2 jit_solution(1703413751848722447)
XLA Ops:
  0.7 0.9 reduce-window.8
  1.5 0.1 fusion.13
  1.6 0.1 fusion.83
  1.7 0.1 fusion.84
  1.8 0.1 fusion.85
  1.8 0.1 fusion.86
  2.7 1.2 dynamic_slice.10
  4.6 1.5 copy.31
  6.1 0.4 fusion.98
  6.5 0.1 multiply_convert_fusion.3
  7.5 0.4 copy-done.42
  8.0 1.1 fusion.80
  9.1 0.6 fusion.81
  9.7 0.7 fusion.16
  10.5 0.7 fusion.15
  11.3 3.9 %fusion.49 = (f32[256]{0:T(256)S(1)}, f32[256]{0:T(256)S(1)}, f32[256,256]{1,0:T(8,128)S(1)}) fusion(f32[256]{0:T(256)S(1)} %get-tuple-element.142, f32[241,256]{1,0:T(8,128)S(1)} %get-tuple-element.78, f32[256]{0:T(256)} %bitcast.33, f32[256]{0:T(256)S(1)} %get-tuple-element.143, f32[242,256]{1,0:T(8,128)S(1)} %get-tuple-element.80, f32[256]{0:T(256)} %bitcast.32, ...), kind=kLoop, calls=%fused_computation.171 | loop fusion | flops 6290944 | bytes 8077312 | tf_op jit(solution)/shard_map/reduce_sum | solution.py:73
  15.5 0.6 pad_maximum_fusion.4
  16.1 3.1 %psum.35 = f32[2,256]{1,0:T(2,128)} all-reduce(f32[2,256]{1,0:T(2,128)} %pad_maximum_fusion.4), channel_id=1, replica_groups=mesh['y'=8,'z'=8,'core'=2,'mp'=4] {'core'}, use_global_device_ids=true, to_apply=%region_4.5 | all-reduce | flops 512 | bytes 4096 | tf_op jit(solution)/shard_map/psum | solution.py:28
  19.2 1.4 broadcast_in_dim.4
  20.6 16.8 %all-to-all-start = ((f32[64,2,256]{2,1,0:T(2,128)}), f32[64,2,256]{2,1,0:T(2,128)}, u32[]{:S(2)}, u32[]{:S(2)}) async-start(f32[64,2,256]{2,1,0:T(2,128)} %broadcast_in_dim.4), calls=%async_computation | async-start | bytes 262144 | tf_op jit(solution)/shard_map/all_to_all | solution.py:31
  37.5 1.3 reduce_sum.376
  39.4 10.9 %all-to-all-done = f32[64,2,256]{2,1,0:T(2,128)} async-done(((f32[64,2,256]{2,1,0:T(2,128)}), f32[64,2,256]{2,1,0:T(2,128)}, u32[]{:S(2)}, u32[]{:S(2)}) %all-to-all-start) | async-done | bytes 131104 | tf_op jit(solution)/shard_map/all_to_all | solution.py:31
  50.3 1.6 reduce_sum.375
  51.8 0.8 add_rsqrt_fusion
  52.6 0.6 copy-done.71
  53.2 2.2 %fusion.48 = (f32[256]{0:T(256)S(1)}, f32[256]{0:T(256)S(1)}, f32[256,256]{1,0:T(8,128)}) fusion(f32[256]{0:T(256)S(1)} %bitcast.118, f32[256,256]{1,0:T(8,128)S(1)} %get-tuple-element.46, f32[256]{0:T(256)S(1)} %bitcast.121, f32[256]{0:T(256)} %param.13, f32[256]{0:T(256)} %param.12, f32[256]{0:T(256)S(1)} %fusion.44, bf16[256,1024]{1,0:T(8,128)(2,1)} %param.15, ...), kind=kOutput, calls=%fused_computation.170 | convolution fusion | flops 135265792 | bytes 1580032 | tf_op jit(solution)/shard_map/dot_general | solution.py:82
  55.4 0.6 pad_maximum_fusion.5
  56.0 3.1 %psum.36 = f32[2,256]{1,0:T(2,128)} all-reduce(f32[2,256]{1,0:T(2,128)} %pad_maximum_fusion.5), channel_id=1, replica_groups=mesh['y'=8,'z'=8,'core'=2,'mp'=4] {'core'}, use_global_device_ids=true, to_apply=%region_9.10 | all-reduce | flops 512 | bytes 4096 | tf_op jit(solution)/shard_map/psum | solution.py:28
  59.2 1.4 broadcast_in_dim.5
  60.5 5.4 %all-to-all-start.1 = ((f32[64,2,256]{2,1,0:T(2,128)}), f32[64,2,256]{2,1,0:T(2,128)}, u32[]{:S(2)}, u32[]{:S(2)}) async-start(f32[64,2,256]{2,1,0:T(2,128)} %broadcast_in_dim.5), calls=%async_computation.1 | async-start | bytes 262144 | tf_op jit(solution)/shard_map/all_to_all | solution.py:31
  66.0 2.5 %convolution_bitcast_fusion.1 = f32[1024,256]{0,1:T(8,128)} fusion(bf16[256,1024]{1,0:T(8,128)(2,1)} %param.15, f32[256,256]{1,0:T(8,128)S(1)} %get-tuple-element.46, f32[256]{0:T(256)} %param.13, f32[256]{0:T(256)} %bitcast.122, f32[256]{0:T(256)} %bitcast.119, f32[256]{0:T(256)} %param.12, f32[256]{0:T(256)S(1)} %fusion.44), kind=kOutput, calls=%fused_computation.6 | convolution fusion | flops 134873088 | bytes 1840128 | tf_op jit(solution)/shard_map/dot_general | solution.py:121
  68.5 10.7 %all-to-all-done.1 = f32[64,2,256]{2,1,0:T(2,128)} async-done(((f32[64,2,256]{2,1,0:T(2,128)}), f32[64,2,256]{2,1,0:T(2,128)}, u32[]{:S(2)}, u32[]{:S(2)}) %all-to-all-start.1) | async-done | bytes 131104 | tf_op jit(solution)/shard_map/all_to_all | solution.py:31
  79.2 1.6 reduce_sum.379
  80.7 1.3 fusion.82
  82.1 2.9 %multiply_reduce_fusion = (f32[256]{0:T(256)}, f32[256]{0:T(256)}, f32[256]{0:T(256)}, f32[256]{0:T(256)}, f32[256]{0:T(256)}, /*index=5*/f32[256]{0:T(256)}, f3...) fusion(f32[241,256]{1,0:T(8,128)} %copy-done.28, f32[256]{0:T(256)S(1)} %get-tuple-element.142, ...), kind=kLoop, calls=%fused_computation.18 | loop fusion | flops 2356992 | bytes 3068932 | tf_op jit(solution)/shard_map/reduce_sum | solution.py:96
  85.8 0.3 copy-done.44
  86.2 3.9 %multiply_convert_fusion.2 = (bf16[256,256]{1,0:T(8,128)(2,1)S(1)}, f32[256,256]{1,0:T(8,128)S(1)}) fusion(f32[256,512]{1,0:T(8,128)S(1)} %fusion.98, f32[256]{0:T(256)} %get-tuple-element.172, f32[241,256]{1,0:T(8,128)S(1)} %get-tuple-element.48, f32[256]{0:T(256)} %bitcast.33, f32[256]{0:T(256)} %get-tuple-element.141, ...), kind=kLoop, calls=%fused_computation.51 | loop fusion | flops 6356992 | bytes 8599552 | tf_op jit(solution)/shard_map/convert.1
  90.1 0.1 multiply_convert_fusion.1
  90.2 0.5 copy-done.39
  90.7 0.1 copy-done.38
  90.9 0.5 convolution_bitcast_fusion
  91.3 0.1 copy-done.41
  91.4 1.9 pad_maximum_fusion
  93.3 3.5 %copy.23 = f32[1024,768]{1,0:T(8,128)} copy(f32[1024,768]{0,1:T(8,128)} %pad_maximum_fusion) | data formatting | bytes 6291456 | tf_op jit(solution)/shard_map/concatenate | solution.py:116
  96.9 2.4 %fusion.3 = bf16[64,8,768]{2,1,0:T(8,128)(2,1)} fusion(f32[64,2,8,768]{3,2,1,0:T(8,128)} %bitcast.101, s32[]{:T(128)S(6)} %select_n.12), kind=kLoop, calls=%fused_computation.11 | loop fusion | bytes 1572868 | tf_op jit(solution)/shard_map/convert_element_type | solution.py:40
  99.3 1.9 collective-permute-start
  101.2 1.4 convolution_convert_fusion
  102.6 0.9 copy.33
  103.5 4.8 %all-to-all-start.2 = ((bf16[4,256,256]{2,1,0:T(8,128)(2,1)}), bf16[4,256,256]{2,1,0:T(8,128)(2,1)S(1)}, u32[]{:S(2)}, u32[]{:S(2)}) async-start(bf16[4,256,256]{2,1,0:T(8,128)(2,1)} %bitcast.100), calls=%async_computation.2 | async-start | bytes 1048576 | tf_op jit(solution)/shard_map/all_to_all | solution.py:113
  108.3 2.7 %fusion = bf16[64,8,768]{2,1,0:T(8,128)(2,1)} fusion(bf16[64,8,768]{2,1,0:T(8,128)(2,1)} %collective-permute-done, f32[64,2,8,768]{3,2,1,0:T(8,128)} %bitcast.102, s32[]{:T(128)S(6)} %select_n.11), kind=kLoop, calls=%fused_computation.3 | loop fusion | flops 1179648 | bytes 3145732 | tf_op jit(solution)/shard_map/convert_element_type | solution.py:42
  111.0 5.9 %all-to-all-done.2 = bf16[4,256,256]{2,1,0:T(8,128)(2,1)S(1)} async-done(((bf16[4,256,256]{2,1,0:T(8,128)(2,1)}), bf16[4,256,256]{2,1,0:T(8,128)(2,1)S(1)}, u32[]{:S(2)}, u32[]{:S(2)}) %all-to-all-start.2) | async-done | bytes 524320 | tf_op jit(solution)/shard_map/all_to_all | solution.py:113
  117.0 0.8 copy-done.36
  117.8 4.8 %all-to-all-start.3 = ((bf16[64,8,768]{2,1,0:T(8,128)(2,1)}), bf16[64,8,768]{2,1,0:T(8,128)(2,1)S(1)}, u32[]{:S(2)}, u32[]{:S(2)}) async-start(bf16[64,8,768]{2,1,0:T(8,128)(2,1)} %fusion), calls=%async_computation.3 | async-start | bytes 1572864 | tf_op jit(solution)/shard_map/all_to_all | solution.py:43
  122.7 2.3 %multiply_reduce_fusion.27 = (f32[256]{0:T(256)}, f32[256]{0:T(256)}, f32[256]{0:T(256)}, f32[256]{0:T(256)}) fusion(f32[256,256]{1,0:T(8,128)S(1)} %get-tuple-element.41, f32[244,256]{1,0:T(8,128)} %copy-done.23, f32[256]{0:T(256)} %get-tuple-element.171, f32[256]{0:T(256)} %get-tuple-element.159, f32[243,256]{1,0:T(8,128)} %copy-done.22, ...), kind=kLoop, calls=%fused_computation.45 | loop fusion | flops 785408 | bytes 1263616 | tf_op jit(solution)/shard_map/reduce_sum | solution.py:96
  125.0 2.5 %multiply_reduce_fusion.18 = (f32[256]{0:T(256)}, f32[256]{0:T(256)}, f32[256]{0:T(256)}, f32[256]{0:T(256)}, f32[256]{0:T(256)}, /*index=5*/f32[256]{0:T(256)}, f32[256]{0:T(256)}, f32[256]{0:T(256)}, f32[256]{0:T(256)}) fusion(f32[256,256]{1,0:T(8,128)S(1)} %get-tuple-element.41, f32[253,256]{1,0:T(8,128)S(1)} %get-tuple-element.101, ...), kind=kLoop, calls=%fused_computation.36 | loop fusion | flops 1767168 | bytes 2575360 | tf_op jit(solution)/shard_map/reduce_sum | solution.py:96
  127.6 1.2 multiply_reduce_fusion.9
  128.8 2.9 %stack.151 = f32[31,256]{1,0:T(8,128)S(1)} concatenate(f32[1,256]{1,0:T(1,128)} %bitcast.128, f32[1,256]{1,0:T(1,128)} %bitcast.127, f32[1,256]{1,0:T(1,128)} %bitcast.126, f32[1,256]{1,0:T(1,128)} %bitcast.125, f32[1,256]{1,0:T(1,128)} %bitcast.137, f32[1,256]{1,0:T(1,128)} %bitcast.136, f32[1,256]{1,0:T(1,128)} %bitcast.135, f32[1,256]{1,0:T(1,128)} %bitcast.134, ...), dimensions={0} | concatenate | bytes 63488 | tf_op jit(solution)/shard_map/stack | solution.py:98
  131.6 3.4 %psum.37 = f32[31,256]{1,0:T(8,128)S(1)} all-reduce(f32[31,256]{1,0:T(8,128)S(1)} %stack.151), channel_id=1, replica_groups=mesh['y'=8,'z'=8,'core'=2,'mp'=4] {'core'}, use_global_device_ids=true, to_apply=%region_44.45 | all-reduce | flops 7936 | bytes 63488 | tf_op jit(solution)/shard_map/psum | solution.py:98
  135.1 29.8 %psum.38 = f32[31,256]{1,0:T(8,128)S(1)} all-reduce(f32[31,256]{1,0:T(8,128)S(1)} %psum.37), channel_id=1, replica_groups=mesh['y'=8,'z'=8,'core'=2,'mp'=4] {'y'}, use_global_device_ids=true, to_apply=%region_45.46 | all-reduce | flops 7936 | bytes 63488 | tf_op jit(solution)/shard_map/psum | solution.py:98
  164.8 30.2 %psum.39 = f32[31,256]{1,0:T(8,128)} all-reduce(f32[31,256]{1,0:T(8,128)S(1)} %psum.38), channel_id=1, replica_groups=mesh['y'=8,'z'=8,'core'=2,'mp'=4] {'z'}, use_global_device_ids=true, to_apply=%region_46.47 | all-reduce | flops 7936 | bytes 63488 | tf_op jit(solution)/shard_map/psum | solution.py:98
  195.0 0.7 reduce_sum.380
  195.8 0.1 convert_reduce_fusion
  195.9 0.6 slice.684
  196.5 0.6 reshape.163
  (184 shorter events, 2.2 us)
Async XLA Ops:
  0.6 5.4 %copy-start = (bf16[256,1024]{1,0:T(8,128)(2,1)S(1)}, bf16[256,1024]{1,0:T(8,128)(2,1)}, u32[]{:S(2)}) copy-start(bf16[256,1024]{1,0:T(8,128)(2,1)} %param.9) | copy-start | bytes 1572868
  6.7 4.5 %copy-start.4 = (f32[252,256]{1,0:T(8,128)}, f32[252,256]{1,0:T(8,128)S(1)}, u32[]{:S(2)}) copy-start(f32[252,256]{1,0:T(8,128)S(1)} %get-tuple-element.100) | copy-start | bytes 774148
  6.7 4.5 %copy-start.6 = (f32[253,256]{1,0:T(8,128)}, f32[253,256]{1,0:T(8,128)S(1)}, u32[]{:S(2)}) copy-start(f32[253,256]{1,0:T(8,128)S(1)} %get-tuple-element.102) | copy-start | bytes 777220
  6.8 4.4 %copy-start.8 = (f32[254,256]{1,0:T(8,128)}, f32[254,256]{1,0:T(8,128)S(1)}, u32[]{:S(2)}) copy-start(f32[254,256]{1,0:T(8,128)S(1)} %get-tuple-element.103) | copy-start | bytes 780292
  6.8 4.4 %copy-start.10 = (f32[254,256]{1,0:T(8,128)}, f32[254,256]{1,0:T(8,128)S(1)}, u32[]{:S(2)}) copy-start(f32[254,256]{1,0:T(8,128)S(1)} %get-tuple-element.104) | copy-start | bytes 780292
  6.8 4.4 %copy-start.12 = (f32[255,256]{1,0:T(8,128)}, f32[255,256]{1,0:T(8,128)S(1)}, u32[]{:S(2)}) copy-start(f32[255,256]{1,0:T(8,128)S(1)} %get-tuple-element.105) | copy-start | bytes 783364
  6.9 4.4 %copy-start.14 = (f32[255,256]{1,0:T(8,128)}, f32[255,256]{1,0:T(8,128)S(1)}, u32[]{:S(2)}) copy-start(f32[255,256]{1,0:T(8,128)S(1)} %get-tuple-element.106) | copy-start | bytes 783364
  6.9 4.3 %copy-start.3 = (f32[249,256]{1,0:T(8,128)}, f32[249,256]{1,0:T(8,128)S(1)}, u32[]{:S(2)}) copy-start(f32[249,256]{1,0:T(8,128)S(1)} %get-tuple-element.94) | copy-start | bytes 764932
  7.0 4.3 %copy-start.16 = (f32[250,256]{1,0:T(8,128)}, f32[250,256]{1,0:T(8,128)S(1)}, u32[]{:S(2)}) copy-start(f32[250,256]{1,0:T(8,128)S(1)} %get-tuple-element.96) | copy-start | bytes 768004
  7.0 4.2 %copy-start.1 = (f32[251,256]{1,0:T(8,128)}, f32[251,256]{1,0:T(8,128)S(1)}, u32[]{:S(2)}) copy-start(f32[251,256]{1,0:T(8,128)S(1)} %get-tuple-element.97) | copy-start | bytes 771076
  7.0 4.2 %copy-start.18 = (f32[251,256]{1,0:T(8,128)}, f32[251,256]{1,0:T(8,128)S(1)}, u32[]{:S(2)}) copy-start(f32[251,256]{1,0:T(8,128)S(1)} %get-tuple-element.98) | copy-start | bytes 771076
  7.1 4.2 %copy-start.20 = (f32[241,256]{1,0:T(8,128)}, f32[241,256]{1,0:T(8,128)S(1)}, u32[]{:S(2)}) copy-start(f32[241,256]{1,0:T(8,128)S(1)} %get-tuple-element.77) | copy-start | bytes 740356
  7.1 4.2 %copy-start.28 = (f32[241,256]{1,0:T(8,128)}, f32[241,256]{1,0:T(8,128)S(1)}, u32[]{:S(2)}) copy-start(f32[241,256]{1,0:T(8,128)S(1)} %get-tuple-element.78) | copy-start | bytes 740356
  7.1 4.2 %copy-start.21 = (f32[242,256]{1,0:T(8,128)}, f32[242,256]{1,0:T(8,128)S(1)}, u32[]{:S(2)}) copy-start(f32[242,256]{1,0:T(8,128)S(1)} %get-tuple-element.79) | copy-start | bytes 743428
  7.2 4.2 %copy-start.29 = (f32[242,256]{1,0:T(8,128)}, f32[242,256]{1,0:T(8,128)S(1)}, u32[]{:S(2)}) copy-start(f32[242,256]{1,0:T(8,128)S(1)} %get-tuple-element.80) | copy-start | bytes 743428
  7.2 0.8 copy-start.42
  7.2 8.0 %copy-start.22 = (f32[243,256]{1,0:T(8,128)}, f32[243,256]{1,0:T(8,128)S(1)}, u32[]{:S(2)}) copy-start(f32[243,256]{1,0:T(8,128)S(1)} %get-tuple-element.81) | copy-start | bytes 746500
  7.2 8.0 %copy-start.30 = (f32[243,256]{1,0:T(8,128)}, f32[243,256]{1,0:T(8,128)S(1)}, u32[]{:S(2)}) copy-start(f32[243,256]{1,0:T(8,128)S(1)} %get-tuple-element.82) | copy-start | bytes 746500
  7.3 7.9 %copy-start.23 = (f32[244,256]{1,0:T(8,128)}, f32[244,256]{1,0:T(8,128)S(1)}, u32[]{:S(2)}) copy-start(f32[244,256]{1,0:T(8,128)S(1)} %get-tuple-element.83) | copy-start | bytes 749572
  7.3 7.9 %copy-start.31 = (f32[244,256]{1,0:T(8,128)}, f32[244,256]{1,0:T(8,128)S(1)}, u32[]{:S(2)}) copy-start(f32[244,256]{1,0:T(8,128)S(1)} %get-tuple-element.84) | copy-start | bytes 749572
  7.4 7.9 %copy-start.24 = (f32[245,256]{1,0:T(8,128)}, f32[245,256]{1,0:T(8,128)S(1)}, u32[]{:S(2)}) copy-start(f32[245,256]{1,0:T(8,128)S(1)} %get-tuple-element.85) | copy-start | bytes 752644
  7.4 7.9 %copy-start.32 = (f32[245,256]{1,0:T(8,128)}, f32[245,256]{1,0:T(8,128)S(1)}, u32[]{:S(2)}) copy-start(f32[245,256]{1,0:T(8,128)S(1)} %get-tuple-element.86) | copy-start | bytes 752644
  7.4 7.9 %copy-start.25 = (f32[246,256]{1,0:T(8,128)}, f32[246,256]{1,0:T(8,128)S(1)}, u32[]{:S(2)}) copy-start(f32[246,256]{1,0:T(8,128)S(1)} %get-tuple-element.87) | copy-start | bytes 755716
  7.4 7.9 %copy-start.33 = (f32[246,256]{1,0:T(8,128)}, f32[246,256]{1,0:T(8,128)S(1)}, u32[]{:S(2)}) copy-start(f32[246,256]{1,0:T(8,128)S(1)} %get-tuple-element.88) | copy-start | bytes 755716
  7.5 7.8 %copy-start.26 = (f32[247,256]{1,0:T(8,128)}, f32[247,256]{1,0:T(8,128)S(1)}, u32[]{:S(2)}) copy-start(f32[247,256]{1,0:T(8,128)S(1)} %get-tuple-element.89) | copy-start | bytes 758788
  7.5 7.8 %copy-start.34 = (f32[247,256]{1,0:T(8,128)}, f32[247,256]{1,0:T(8,128)S(1)}, u32[]{:S(2)}) copy-start(f32[247,256]{1,0:T(8,128)S(1)} %get-tuple-element.90) | copy-start | bytes 758788
  8.0 7.3 %copy-start.27 = (f32[248,256]{1,0:T(8,128)}, f32[248,256]{1,0:T(8,128)S(1)}, u32[]{:S(2)}) copy-start(f32[248,256]{1,0:T(8,128)S(1)} %get-tuple-element.91) | copy-start | bytes 761860
  8.0 7.4 %copy-start.35 = (f32[248,256]{1,0:T(8,128)}, f32[248,256]{1,0:T(8,128)S(1)}, u32[]{:S(2)}) copy-start(f32[248,256]{1,0:T(8,128)S(1)} %get-tuple-element.92) | copy-start | bytes 761860
  10.4 4.9 %copy-start.55 = (f32[256]{0:T(256)}, f32[256]{0:T(256)S(1)}, u32[]{:S(2)}) copy-start(f32[256]{0:T(256)S(1)} %get-tuple-element.160) | copy-start | bytes 3076
  10.4 4.9 %copy-start.58 = (f32[256]{0:T(256)}, f32[256]{0:T(256)S(1)}, u32[]{:S(2)}) copy-start(f32[256]{0:T(256)S(1)} %get-tuple-element.161) | copy-start | bytes 3076
  10.4 4.9 %copy-start.61 = (f32[256]{0:T(256)}, f32[256]{0:T(256)S(1)}, u32[]{:S(2)}) copy-start(f32[256]{0:T(256)S(1)} %get-tuple-element.162) | copy-start | bytes 3076
  10.4 4.9 %copy-start.64 = (f32[256]{0:T(256)}, f32[256]{0:T(256)S(1)}, u32[]{:S(2)}) copy-start(f32[256]{0:T(256)S(1)} %get-tuple-element.163) | copy-start | bytes 3076
  10.5 4.9 %copy-start.66 = (f32[256]{0:T(256)}, f32[256]{0:T(256)S(1)}, u32[]{:S(2)}) copy-start(f32[256]{0:T(256)S(1)} %get-tuple-element.164) | copy-start | bytes 3076
  10.5 4.9 %copy-start.68 = (f32[256]{0:T(256)}, f32[256]{0:T(256)S(1)}, u32[]{:S(2)}) copy-start(f32[256]{0:T(256)S(1)} %get-tuple-element.165) | copy-start | bytes 3076
  11.1 4.3 %copy-start.43 = (f32[256]{0:T(256)}, f32[256]{0:T(256)S(1)}, u32[]{:S(2)}) copy-start(f32[256]{0:T(256)S(1)} %get-tuple-element.145) | copy-start | bytes 3076
  11.1 4.3 %copy-start.45 = (f32[256]{0:T(256)}, f32[256]{0:T(256)S(1)}, u32[]{:S(2)}) copy-start(f32[256]{0:T(256)S(1)} %get-tuple-element.146) | copy-start | bytes 3076
  11.1 4.3 %copy-start.47 = (f32[256]{0:T(256)}, f32[256]{0:T(256)S(1)}, u32[]{:S(2)}) copy-start(f32[256]{0:T(256)S(1)} %get-tuple-element.147) | copy-start | bytes 3076
  11.1 4.3 %copy-start.49 = (f32[256]{0:T(256)}, f32[256]{0:T(256)S(1)}, u32[]{:S(2)}) copy-start(f32[256]{0:T(256)S(1)} %get-tuple-element.148) | copy-start | bytes 3076
  11.2 4.3 %copy-start.51 = (f32[256]{0:T(256)}, f32[256]{0:T(256)S(1)}, u32[]{:S(2)}) copy-start(f32[256]{0:T(256)S(1)} %get-tuple-element.149) | copy-start | bytes 3076
  11.2 4.3 %copy-start.53 = (f32[256]{0:T(256)}, f32[256]{0:T(256)S(1)}, u32[]{:S(2)}) copy-start(f32[256]{0:T(256)S(1)} %get-tuple-element.150) | copy-start | bytes 3076
  15.4 66.6 %copy-start.40 = (f32[256,256]{1,0:T(8,128)}, f32[256,256]{1,0:T(8,128)S(1)}, u32[]{:S(2)}) copy-start(f32[256,256]{1,0:T(8,128)S(1)} %get-tuple-element.46) | copy-start | bytes 786436
  20.6 29.7 %all-to-all-start = ((f32[64,2,256]{2,1,0:T(2,128)}), f32[64,2,256]{2,1,0:T(2,128)}, u32[]{:S(2)}, u32[]{:S(2)}) async-start(f32[64,2,256]{2,1,0:T(2,128)} %broadcast_in_dim.4), calls=%async_computation | async-start | bytes 262144 | tf_op jit(solution)/shard_map/all_to_all | solution.py:31
  52.6 2.8 %copy-start.72 = (f32[1,256]{1,0:T(1,128)}, f32[1,256]{1,0:T(1,128)S(1)}, u32[]{:S(2)}) copy-start(f32[1,256]{1,0:T(1,128)S(1)} %get-tuple-element.45) | copy-start | bytes 3076
  60.5 18.7 %all-to-all-start.1 = ((f32[64,2,256]{2,1,0:T(2,128)}), f32[64,2,256]{2,1,0:T(2,128)}, u32[]{:S(2)}, u32[]{:S(2)}) async-start(f32[64,2,256]{2,1,0:T(2,128)} %broadcast_in_dim.5), calls=%async_computation.1 | async-start | bytes 262144 | tf_op jit(solution)/shard_map/all_to_all | solution.py:31
  82.1 3.1 %copy-start.70 = (f32[1,256]{1,0:T(1,128)}, f32[1,256]{1,0:T(1,128)S(1)}, u32[]{:S(2)}) copy-start(f32[1,256]{1,0:T(1,128)S(1)} %get-tuple-element.140) | copy-start | bytes 3076
  85.4 0.7 copy-start.48
  90.1 1.3 copy-start.41
  99.3 9.0 %collective-permute-start = (bf16[64,8,768]{2,1,0:T(8,128)(2,1)}, bf16[64,8,768]{2,1,0:T(8,128)(2,1)}, u32[]{:S(2)}, u32[]{:S(2)}) collective-permute-start(bf16[64,8,768]{2,1,0:T(8,128)(2,1)} %fusion.3), channel_id=1, source_target_pairs={{0,4},{4,0},{1,5},{5,1},{2,6},{6,2},{3,7},{7,3},{8,12},{12,8},{9,1... | collective-permute-start | bytes 2359304 | tf_op jit(solution)/shard_map/ppermute | solution.py:41
  103.5 13.5 %all-to-all-start.2 = ((bf16[4,256,256]{2,1,0:T(8,128)(2,1)}), bf16[4,256,256]{2,1,0:T(8,128)(2,1)S(1)}, u32[]{:S(2)}, u32[]{:S(2)}) async-start(bf16[4,256,256]{2,1,0:T(8,128)(2,1)} %bitcast.100), calls=%async_computation.2 | async-start | bytes 1048576 | tf_op jit(solution)/shard_map/all_to_all | solution.py:113
  108.3 16.7 %copy-start.2 = (f32[251,256]{1,0:T(8,128)S(1)}, f32[251,256]{1,0:T(8,128)}, u32[]{:S(2)}) copy-start(f32[251,256]{1,0:T(8,128)} %copy-done.1) | copy-start | bytes 771076
  108.3 16.7 %copy-start.63 = (f32[256]{0:T(256)S(1)}, f32[256]{0:T(256)}, u32[]{:S(2)}) copy-start(f32[256]{0:T(256)} %copy-done.61) | copy-start | bytes 3076
  111.0 16.5 %copy-start.5 = (f32[252,256]{1,0:T(8,128)S(1)}, f32[252,256]{1,0:T(8,128)}, u32[]{:S(2)}) copy-start(f32[252,256]{1,0:T(8,128)} %copy-done.4) | copy-start | bytes 774148
  111.0 16.5 %copy-start.7 = (f32[253,256]{1,0:T(8,128)S(1)}, f32[253,256]{1,0:T(8,128)}, u32[]{:S(2)}) copy-start(f32[253,256]{1,0:T(8,128)} %copy-done.6) | copy-start | bytes 777220
  111.0 16.5 %copy-start.57 = (f32[256]{0:T(256)S(1)}, f32[256]{0:T(256)}, u32[]{:S(2)}) copy-start(f32[256]{0:T(256)} %copy-done.55) | copy-start | bytes 3076
  111.0 16.5 %copy-start.60 = (f32[256]{0:T(256)S(1)}, f32[256]{0:T(256)}, u32[]{:S(2)}) copy-start(f32[256]{0:T(256)} %copy-done.58) | copy-start | bytes 3076
  117.0 0.8 copy-start.36
  117.8 78.0 %all-to-all-start.3 = ((bf16[64,8,768]{2,1,0:T(8,128)(2,1)}), bf16[64,8,768]{2,1,0:T(8,128)(2,1)S(1)}, u32[]{:S(2)}, u32[]{:S(2)}) async-start(bf16[64,8,768]{2,1,0:T(8,128)(2,1)} %fusion), calls=%async_computation.3 | async-start | bytes 1572864 | tf_op jit(solution)/shard_map/all_to_all | solution.py:43
  122.6 4.9 %copy-start.9 = (f32[254,256]{1,0:T(8,128)S(1)}, f32[254,256]{1,0:T(8,128)}, u32[]{:S(2)}) copy-start(f32[254,256]{1,0:T(8,128)} %copy-done.8) | copy-start | bytes 780292
  122.6 4.9 %copy-start.11 = (f32[254,256]{1,0:T(8,128)S(1)}, f32[254,256]{1,0:T(8,128)}, u32[]{:S(2)}) copy-start(f32[254,256]{1,0:T(8,128)} %copy-done.10) | copy-start | bytes 780292
  122.6 4.9 %copy-start.13 = (f32[255,256]{1,0:T(8,128)S(1)}, f32[255,256]{1,0:T(8,128)}, u32[]{:S(2)}) copy-start(f32[255,256]{1,0:T(8,128)} %copy-done.12) | copy-start | bytes 783364
  122.6 4.9 %copy-start.15 = (f32[255,256]{1,0:T(8,128)S(1)}, f32[255,256]{1,0:T(8,128)}, u32[]{:S(2)}) copy-start(f32[255,256]{1,0:T(8,128)} %copy-done.14) | copy-start | bytes 783364
  122.6 4.9 %copy-start.17 = (f32[250,256]{1,0:T(8,128)S(1)}, f32[250,256]{1,0:T(8,128)}, u32[]{:S(2)}) copy-start(f32[250,256]{1,0:T(8,128)} %copy-done.16) | copy-start | bytes 768004
  122.6 4.9 %copy-start.19 = (f32[251,256]{1,0:T(8,128)S(1)}, f32[251,256]{1,0:T(8,128)}, u32[]{:S(2)}) copy-start(f32[251,256]{1,0:T(8,128)} %copy-done.18) | copy-start | bytes 771076
  127.6 67.5 %copy-start.37 = (bf16[4,256,256]{2,1,0:T(8,128)(2,1)S(1)}, bf16[4,256,256]{2,1,0:T(8,128)(2,1)}, u32[]{:S(2)}) copy-start(bf16[4,256,256]{2,1,0:T(8,128)(2,1)} %copy-done.36) | copy-start | bytes 1572868
  (14 other events, 9.2 us)
where the time goes:
time: 198 us; the launch traced here: 197 us
  blocking collectives  69.7 us (35%)
  starting transfers between devices  33.9 us (17%)
  other arithmetic  32.5 us (16%)
  waiting for transfers between devices  27.5 us (14%)
  local copies, waits for them, and re-layouts  23.4 us (12%)
  matrix products  7.04 us (4%)
  between operations  3.18 us (2%)
    psum x1, blocking collectives, shards(): lax.psum(lax.psum(lax.psum(jnp.stack(depth_rows), 'core'), 'y'), 'z')  30.2 us
    psum x1, blocking collectives, shards(): lax.psum(lax.psum(jnp.stack(depth_rows), 'core'), 'y')  29.8 us
    all_to_all x2, starting transfers between devices, small_sum(): return jnp.sum(lax.all_to_all(every, ('y', 'z'), 0, 0), axis=0)  22.3 us
    all_to_all x2, waiting for transfers between devices, small_sum(): return jnp.sum(lax.all_to_all(every, ('y', 'z'), 0, 0), axis=0)  21.6 us
    reduce_sum x4, other arithmetic, shards(): jnp.sum(grad_conv * tap_term(glu_float, owner_id, live_col, tap_index - r...  8.92 us
    psum x2, blocking collectives, small_sum(): x = lax.psum(x, 'core')  6.29 us
    all_to_all x1, waiting for transfers between devices, shards(): frame_parts = lax.all_to_all(jnp.swapaxes(frame_parts, 0, 1), 'mp', 0, 0)  5.93 us
    another operation x3, other arithmetic  4.9 us
  transfers between devices with their start and end apart: 5, of which 3 were waited for; matrix products, arithmetic and copies ran while one was open for 9% of the time, Pallas kernels for 0%

commit v1 on v0

--- a/solution.py
+++ b/solution.py
@@ -5,6 +5,12 @@
 
 BLOCK = 128
 DP = ("y", "z", "core")
+
+
+def add_all(x, name):
+    blocks = lax.all_gather(x, name, axis=0, tiled=False)
+    total = blocks.sum(axis=0)
+    return total
 
 
 def time_shift(values, offset, fill_value):
@@ -95,7 +101,7 @@
         depth_rows.append(
             jnp.sum(grad_conv * tap_term(glu_float, owner_id, live_col, tap_index - radius), axis=0)
         )
-    depth_grad = lax.psum(lax.psum(lax.psum(jnp.stack(depth_rows), "core"), "y"), "z")
+    depth_grad = lax.psum(lax.psum(add_all(jnp.stack(depth_rows), "core"), "y"), "z")
     grad_glu = jnp.zeros((frames_dev, channels), jnp.float32)
     for tap_index in range(tap_count):
         offset = tap_index - radius

time: 198 us -> 198 us (level)
    psum x3 -> x2, blocking collectives: 63.4 us -> 60.8 us  [the longest x1 30.6 us: shards(): lax.psum(add_all(jnp.stack(depth_rows), 'core'), 'y')]
where the time goes in v1:
time: 198 us; the launch traced here: 196 us
  blocking collectives  69 us (35%)
  starting transfers between devices  33.7 us (17%)
  other arithmetic  32.5 us (16%)
  waiting for transfers between devices  27.5 us (14%)
  local copies, waits for them, and re-layouts  23.4 us (12%)
  matrix products  7.04 us (4%)
  between operations  3.17 us (2%)
    psum x1, blocking collectives, shards(): lax.psum(add_all(jnp.stack(depth_rows), 'core'), 'y')  30.6 us
    psum x1, blocking collectives, shards(): lax.psum(lax.psum(add_all(jnp.stack(depth_rows), 'core'), 'y'), 'z')  30.2 us
    all_to_all x2, starting transfers between devices, small_sum(): return jnp.sum(lax.all_to_all(every, ('y', 'z'), 0, 0), axis=0)  22.3 us
    all_to_all x2, waiting for transfers between devices, small_sum(): return jnp.sum(lax.all_to_all(every, ('y', 'z'), 0, 0), axis=0)  21.6 us
    reduce_sum x4, other arithmetic, shards(): jnp.sum(grad_conv * tap_term(glu_float, owner_id, live_col, tap_index - r...  8.92 us
    psum x2, blocking collectives, small_sum(): x = lax.psum(x, 'core')  6.29 us
    all_to_all x1, waiting for transfers between devices, shards(): frame_parts = lax.all_to_all(jnp.swapaxes(frame_parts, 0, 1), 'mp', 0, 0)  5.93 us
    another operation x3, other arithmetic  4.9 us
  transfers between devices with their start and end apart: 5, of which 3 were waited for; matrix products, arithmetic and copies ran while one was open for 9% of the time, Pallas kernels for 0%

profile of v1, /device:TPU:2, one launch (start us, length us, event | category | flops | bytes accessed | tf_op | source)
XLA Modules:
  0.0 196.3 jit_solution(1570528652343166006)
XLA Ops:
  0.7 0.9 reduce-window.8
  1.5 0.1 fusion.13
  1.6 0.1 fusion.83
  1.7 0.1 fusion.84
  1.8 0.1 fusion.85
  1.8 0.1 fusion.86
  2.7 1.2 dynamic_slice.10
  4.6 1.5 copy.31
  6.1 0.4 fusion.98
  6.5 0.1 multiply_convert_fusion.3
  7.5 0.4 copy-done.42
  8.0 1.1 fusion.80
  9.1 0.6 fusion.81
  9.7 0.7 fusion.16
  10.5 0.7 fusion.15
  11.3 3.9 %fusion.49 = (f32[256]{0:T(256)S(1)}, f32[256]{0:T(256)S(1)}, f32[256,256]{1,0:T(8,128)S(1)}) fusion(f32[256]{0:T(256)S(1)} %get-tuple-element.142, f32[241,256]{1,0:T(8,128)S(1)} %get-tuple-element.78, f32[256]{0:T(256)} %bitcast.33, f32[256]{0:T(256)S(1)} %get-tuple-element.143, f32[242,256]{1,0:T(8,128)S(1)} %get-tuple-element.80, f32[256]{0:T(256)} %bitcast.32, ...), kind=kLoop, calls=%fused_computation.171 | loop fusion | flops 6290944 | bytes 8077312 | tf_op jit(solution)/shard_map/reduce_sum | solution.py:79
  15.5 0.6 pad_maximum_fusion.4
  16.1 3.1 %psum.28 = f32[2,256]{1,0:T(2,128)} all-reduce(f32[2,256]{1,0:T(2,128)} %pad_maximum_fusion.4), channel_id=1, replica_groups=mesh['y'=8,'z'=8,'core'=2,'mp'=4] {'core'}, use_global_device_ids=true, to_apply=%region_4.5 | all-reduce | flops 512 | bytes 4096 | tf_op jit(solution)/shard_map/psum | solution.py:34
  19.2 1.4 broadcast_in_dim.4
  20.6 16.9 %all-to-all-start = ((f32[64,2,256]{2,1,0:T(2,128)}), f32[64,2,256]{2,1,0:T(2,128)}, u32[]{:S(2)}, u32[]{:S(2)}) async-start(f32[64,2,256]{2,1,0:T(2,128)} %broadcast_in_dim.4), calls=%async_computation | async-start | bytes 262144 | tf_op jit(solution)/shard_map/all_to_all | solution.py:37
  37.5 1.3 reduce_sum.385
  39.4 10.9 %all-to-all-done = f32[64,2,256]{2,1,0:T(2,128)} async-done(((f32[64,2,256]{2,1,0:T(2,128)}), f32[64,2,256]{2,1,0:T(2,128)}, u32[]{:S(2)}, u32[]{:S(2)}) %all-to-all-start) | async-done | bytes 131104 | tf_op jit(solution)/shard_map/all_to_all | solution.py:37
  50.3 1.6 reduce_sum.384
  51.8 0.8 add_rsqrt_fusion
  52.6 0.6 copy-done.71
  53.2 2.2 %fusion.48 = (f32[256]{0:T(256)S(1)}, f32[256]{0:T(256)S(1)}, f32[256,256]{1,0:T(8,128)}) fusion(f32[256]{0:T(256)S(1)} %bitcast.120, f32[256,256]{1,0:T(8,128)S(1)} %get-tuple-element.46, f32[256]{0:T(256)S(1)} %bitcast.123, f32[256]{0:T(256)} %param.13, f32[256]{0:T(256)} %param.12, f32[256]{0:T(256)S(1)} %fusion.44, bf16[256,1024]{1,0:T(8,128)(2,1)} %param.15, ...), kind=kOutput, calls=%fused_computation.170 | convolution fusion | flops 135265792 | bytes 1580032 | tf_op jit(solution)/shard_map/dot_general | solution.py:88
  55.4 0.6 pad_maximum_fusion.5
  56.0 3.1 %psum.29 = f32[2,256]{1,0:T(2,128)} all-reduce(f32[2,256]{1,0:T(2,128)} %pad_maximum_fusion.5), channel_id=1, replica_groups=mesh['y'=8,'z'=8,'core'=2,'mp'=4] {'core'}, use_global_device_ids=true, to_apply=%region_9.10 | all-reduce | flops 512 | bytes 4096 | tf_op jit(solution)/shard_map/psum | solution.py:34
  59.2 1.4 broadcast_in_dim.5
  60.5 5.4 %all-to-all-start.1 = ((f32[64,2,256]{2,1,0:T(2,128)}), f32[64,2,256]{2,1,0:T(2,128)}, u32[]{:S(2)}, u32[]{:S(2)}) async-start(f32[64,2,256]{2,1,0:T(2,128)} %broadcast_in_dim.5), calls=%async_computation.1 | async-start | bytes 262144 | tf_op jit(solution)/shard_map/all_to_all | solution.py:37
  66.0 2.5 %convolution_bitcast_fusion.1 = f32[1024,256]{0,1:T(8,128)} fusion(bf16[256,1024]{1,0:T(8,128)(2,1)} %param.15, f32[256,256]{1,0:T(8,128)S(1)} %get-tuple-element.46, f32[256]{0:T(256)} %param.13, f32[256]{0:T(256)} %bitcast.124, f32[256]{0:T(256)} %bitcast.121, f32[256]{0:T(256)} %param.12, f32[256]{0:T(256)S(1)} %fusion.44), kind=kOutput, calls=%fused_computation.6 | convolution fusion | flops 134873088 | bytes 1840128 | tf_op jit(solution)/shard_map/dot_general | solution.py:127
  68.5 10.7 %all-to-all-done.1 = f32[64,2,256]{2,1,0:T(2,128)} async-done(((f32[64,2,256]{2,1,0:T(2,128)}), f32[64,2,256]{2,1,0:T(2,128)}, u32[]{:S(2)}, u32[]{:S(2)}) %all-to-all-start.1) | async-done | bytes 131104 | tf_op jit(solution)/shard_map/all_to_all | solution.py:37
  79.2 1.6 reduce_sum.388
  80.8 1.3 fusion.82
  82.1 2.9 %multiply_reduce_fusion = (f32[256]{0:T(256)}, f32[256]{0:T(256)}, f32[256]{0:T(256)}, f32[256]{0:T(256)}, f32[256]{0:T(256)}, /*index=5*/f32[256]{0:T(256)}, f3...) fusion(f32[241,256]{1,0:T(8,128)} %copy-done.28, f32[256]{0:T(256)S(1)} %get-tuple-element.142, ...), kind=kLoop, calls=%fused_computation.18 | loop fusion | flops 2356992 | bytes 3068932 | tf_op jit(solution)/shard_map/reduce_sum | solution.py:102
  85.8 0.3 copy-done.44
  86.2 3.9 %multiply_convert_fusion.2 = (bf16[256,256]{1,0:T(8,128)(2,1)S(1)}, f32[256,256]{1,0:T(8,128)S(1)}) fusion(f32[256,512]{1,0:T(8,128)S(1)} %fusion.98, f32[256]{0:T(256)} %get-tuple-element.172, f32[241,256]{1,0:T(8,128)S(1)} %get-tuple-element.48, f32[256]{0:T(256)} %bitcast.33, f32[256]{0:T(256)} %get-tuple-element.141, ...), kind=kLoop, calls=%fused_computation.51 | loop fusion | flops 6356992 | bytes 8599552 | tf_op jit(solution)/shard_map/convert.1
  90.1 0.1 multiply_convert_fusion.1
  90.2 0.5 copy-done.39
  90.7 0.1 copy-done.38
  90.9 0.5 convolution_bitcast_fusion
  91.3 0.1 copy-done.41
  91.4 1.9 pad_maximum_fusion
  93.3 3.5 %copy.23 = f32[1024,768]{1,0:T(8,128)} copy(f32[1024,768]{0,1:T(8,128)} %pad_maximum_fusion) | data formatting | bytes 6291456 | tf_op jit(solution)/shard_map/concatenate | solution.py:122
  96.9 2.4 %fusion.3 = bf16[64,8,768]{2,1,0:T(8,128)(2,1)} fusion(f32[64,2,8,768]{3,2,1,0:T(8,128)} %bitcast.102, s32[]{:T(128)S(6)} %select_n.12), kind=kLoop, calls=%fused_computation.11 | loop fusion | bytes 1572868 | tf_op jit(solution)/shard_map/convert_element_type | solution.py:46
  99.3 1.9 collective-permute-start
  101.2 1.4 convolution_convert_fusion
  102.6 0.9 copy.33
  103.5 4.8 %all-to-all-start.2 = ((bf16[4,256,256]{2,1,0:T(8,128)(2,1)}), bf16[4,256,256]{2,1,0:T(8,128)(2,1)S(1)}, u32[]{:S(2)}, u32[]{:S(2)}) async-start(bf16[4,256,256]{2,1,0:T(8,128)(2,1)} %bitcast.101), calls=%async_computation.2 | async-start | bytes 1048576 | tf_op jit(solution)/shard_map/all_to_all | solution.py:119
  108.3 2.7 %fusion = bf16[64,8,768]{2,1,0:T(8,128)(2,1)} fusion(bf16[64,8,768]{2,1,0:T(8,128)(2,1)} %collective-permute-done, f32[64,2,8,768]{3,2,1,0:T(8,128)} %bitcast.103, s32[]{:T(128)S(6)} %select_n.11), kind=kLoop, calls=%fused_computation.3 | loop fusion | flops 1179648 | bytes 3145732 | tf_op jit(solution)/shard_map/convert_element_type | solution.py:48
  111.0 5.9 %all-to-all-done.2 = bf16[4,256,256]{2,1,0:T(8,128)(2,1)S(1)} async-done(((bf16[4,256,256]{2,1,0:T(8,128)(2,1)}), bf16[4,256,256]{2,1,0:T(8,128)(2,1)S(1)}, u32[]{:S(2)}, u32[]{:S(2)}) %all-to-all-start.2) | async-done | bytes 524320 | tf_op jit(solution)/shard_map/all_to_all | solution.py:119
  117.0 0.8 copy-done.36
  117.8 4.6 %all-to-all-start.3 = ((bf16[64,8,768]{2,1,0:T(8,128)(2,1)}), bf16[64,8,768]{2,1,0:T(8,128)(2,1)S(1)}, u32[]{:S(2)}, u32[]{:S(2)}) async-start(bf16[64,8,768]{2,1,0:T(8,128)(2,1)} %fusion), calls=%async_computation.3 | async-start | bytes 1572864 | tf_op jit(solution)/shard_map/all_to_all | solution.py:49
  122.5 2.3 %multiply_reduce_fusion.27 = (f32[256]{0:T(256)}, f32[256]{0:T(256)}, f32[256]{0:T(256)}, f32[256]{0:T(256)}) fusion(f32[256,256]{1,0:T(8,128)S(1)} %get-tuple-element.41, f32[244,256]{1,0:T(8,128)} %copy-done.23, f32[256]{0:T(256)} %get-tuple-element.171, f32[256]{0:T(256)} %get-tuple-element.159, f32[243,256]{1,0:T(8,128)} %copy-done.22, ...), kind=kLoop, calls=%fused_computation.45 | loop fusion | flops 785408 | bytes 1263616 | tf_op jit(solution)/shard_map/reduce_sum | solution.py:102
  124.8 2.5 %multiply_reduce_fusion.18 = (f32[256]{0:T(256)}, f32[256]{0:T(256)}, f32[256]{0:T(256)}, f32[256]{0:T(256)}, f32[256]{0:T(256)}, /*index=5*/f32[256]{0:T(256)}, f32[256]{0:T(256)}, f32[256]{0:T(256)}, f32[256]{0:T(256)}) fusion(f32[256,256]{1,0:T(8,128)S(1)} %get-tuple-element.41, f32[253,256]{1,0:T(8,128)S(1)} %get-tuple-element.101, ...), kind=kLoop, calls=%fused_computation.36 | loop fusion | flops 1767168 | bytes 2575360 | tf_op jit(solution)/shard_map/reduce_sum | solution.py:102
  127.4 1.2 multiply_reduce_fusion.9
  128.6 2.9 %stack.151 = f32[31,256]{1,0:T(8,128)S(1)} concatenate(f32[1,256]{1,0:T(1,128)} %bitcast.130, f32[1,256]{1,0:T(1,128)} %bitcast.129, f32[1,256]{1,0:T(1,128)} %bitcast.128, f32[1,256]{1,0:T(1,128)} %bitcast.127, f32[1,256]{1,0:T(1,128)} %bitcast.139, f32[1,256]{1,0:T(1,128)} %bitcast.138, f32[1,256]{1,0:T(1,128)} %bitcast.137, f32[1,256]{1,0:T(1,128)} %bitcast.136, ...), dimensions={0} | concatenate | bytes 63488 | tf_op jit(solution)/shard_map/stack | solution.py:104
  131.5 1.9 all-gather.1
  133.3 30.6 %psum.30 = f32[31,256]{1,0:T(8,128)S(1)} all-reduce(f32[31,256]{1,0:T(8,128)S(1)} %reduce_sum.422), channel_id=1, replica_groups=mesh['y'=8,'z'=8,'core'=2,'mp'=4] {'y'}, use_global_device_ids=true, to_apply=%region_45.46 | all-reduce | flops 7936 | bytes 63488 | tf_op jit(solution)/shard_map/psum | solution.py:104
  163.9 30.2 %psum.31 = f32[31,256]{1,0:T(8,128)} all-reduce(f32[31,256]{1,0:T(8,128)S(1)} %psum.30), channel_id=1, replica_groups=mesh['y'=8,'z'=8,'core'=2,'mp'=4] {'z'}, use_global_device_ids=true, to_apply=%region_46.47 | all-reduce | flops 7936 | bytes 63488 | tf_op jit(solution)/shard_map/psum | solution.py:104
  194.2 0.7 reduce_sum.389
  194.9 0.1 convert_reduce_fusion
  195.1 0.6 slice.684
  195.7 0.6 reshape.163
  (185 shorter events, 2.2 us)
Async XLA Ops:
  0.6 5.4 %copy-start = (bf16[256,1024]{1,0:T(8,128)(2,1)S(1)}, bf16[256,1024]{1,0:T(8,128)(2,1)}, u32[]{:S(2)}) copy-start(bf16[256,1024]{1,0:T(8,128)(2,1)} %param.9) | copy-start | bytes 1572868
  6.7 4.5 %copy-start.4 = (f32[252,256]{1,0:T(8,128)}, f32[252,256]{1,0:T(8,128)S(1)}, u32[]{:S(2)}) copy-start(f32[252,256]{1,0:T(8,128)S(1)} %get-tuple-element.100) | copy-start | bytes 774148
  6.7 4.5 %copy-start.6 = (f32[253,256]{1,0:T(8,128)}, f32[253,256]{1,0:T(8,128)S(1)}, u32[]{:S(2)}) copy-start(f32[253,256]{1,0:T(8,128)S(1)} %get-tuple-element.102) | copy-start | bytes 777220
  6.8 4.4 %copy-start.8 = (f32[254,256]{1,0:T(8,128)}, f32[254,256]{1,0:T(8,128)S(1)}, u32[]{:S(2)}) copy-start(f32[254,256]{1,0:T(8,128)S(1)} %get-tuple-element.103) | copy-start | bytes 780292
  6.8 4.4 %copy-start.10 = (f32[254,256]{1,0:T(8,128)}, f32[254,256]{1,0:T(8,128)S(1)}, u32[]{:S(2)}) copy-start(f32[254,256]{1,0:T(8,128)S(1)} %get-tuple-element.104) | copy-start | bytes 780292
  6.8 4.4 %copy-start.12 = (f32[255,256]{1,0:T(8,128)}, f32[255,256]{1,0:T(8,128)S(1)}, u32[]{:S(2)}) copy-start(f32[255,256]{1,0:T(8,128)S(1)} %get-tuple-element.105) | copy-start | bytes 783364
  6.9 4.4 %copy-start.14 = (f32[255,256]{1,0:T(8,128)}, f32[255,256]{1,0:T(8,128)S(1)}, u32[]{:S(2)}) copy-start(f32[255,256]{1,0:T(8,128)S(1)} %get-tuple-element.106) | copy-start | bytes 783364
  6.9 4.3 %copy-start.3 = (f32[249,256]{1,0:T(8,128)}, f32[249,256]{1,0:T(8,128)S(1)}, u32[]{:S(2)}) copy-start(f32[249,256]{1,0:T(8,128)S(1)} %get-tuple-element.94) | copy-start | bytes 764932
  7.0 4.3 %copy-start.16 = (f32[250,256]{1,0:T(8,128)}, f32[250,256]{1,0:T(8,128)S(1)}, u32[]{:S(2)}) copy-start(f32[250,256]{1,0:T(8,128)S(1)} %get-tuple-element.96) | copy-start | bytes 768004
  7.0 4.2 %copy-start.1 = (f32[251,256]{1,0:T(8,128)}, f32[251,256]{1,0:T(8,128)S(1)}, u32[]{:S(2)}) copy-start(f32[251,256]{1,0:T(8,128)S(1)} %get-tuple-element.97) | copy-start | bytes 771076
  7.0 4.2 %copy-start.18 = (f32[251,256]{1,0:T(8,128)}, f32[251,256]{1,0:T(8,128)S(1)}, u32[]{:S(2)}) copy-start(f32[251,256]{1,0:T(8,128)S(1)} %get-tuple-element.98) | copy-start | bytes 771076
  7.1 4.2 %copy-start.20 = (f32[241,256]{1,0:T(8,128)}, f32[241,256]{1,0:T(8,128)S(1)}, u32[]{:S(2)}) copy-start(f32[241,256]{1,0:T(8,128)S(1)} %get-tuple-element.77) | copy-start | bytes 740356
  7.1 4.2 %copy-start.28 = (f32[241,256]{1,0:T(8,128)}, f32[241,256]{1,0:T(8,128)S(1)}, u32[]{:S(2)}) copy-start(f32[241,256]{1,0:T(8,128)S(1)} %get-tuple-element.78) | copy-start | bytes 740356
  7.1 4.2 %copy-start.21 = (f32[242,256]{1,0:T(8,128)}, f32[242,256]{1,0:T(8,128)S(1)}, u32[]{:S(2)}) copy-start(f32[242,256]{1,0:T(8,128)S(1)} %get-tuple-element.79) | copy-start | bytes 743428
  7.2 4.2 %copy-start.29 = (f32[242,256]{1,0:T(8,128)}, f32[242,256]{1,0:T(8,128)S(1)}, u32[]{:S(2)}) copy-start(f32[242,256]{1,0:T(8,128)S(1)} %get-tuple-element.80) | copy-start | bytes 743428
  7.2 0.8 copy-start.42
  7.2 8.0 %copy-start.22 = (f32[243,256]{1,0:T(8,128)}, f32[243,256]{1,0:T(8,128)S(1)}, u32[]{:S(2)}) copy-start(f32[243,256]{1,0:T(8,128)S(1)} %get-tuple-element.81) | copy-start | bytes 746500
  7.2 8.0 %copy-start.30 = (f32[243,256]{1,0:T(8,128)}, f32[243,256]{1,0:T(8,128)S(1)}, u32[]{:S(2)}) copy-start(f32[243,256]{1,0:T(8,128)S(1)} %get-tuple-element.82) | copy-start | bytes 746500
  7.3 7.9 %copy-start.23 = (f32[244,256]{1,0:T(8,128)}, f32[244,256]{1,0:T(8,128)S(1)}, u32[]{:S(2)}) copy-start(f32[244,256]{1,0:T(8,128)S(1)} %get-tuple-element.83) | copy-start | bytes 749572
  7.3 7.9 %copy-start.31 = (f32[244,256]{1,0:T(8,128)}, f32[244,256]{1,0:T(8,128)S(1)}, u32[]{:S(2)}) copy-start(f32[244,256]{1,0:T(8,128)S(1)} %get-tuple-element.84) | copy-start | bytes 749572
  7.3 7.9 %copy-start.24 = (f32[245,256]{1,0:T(8,128)}, f32[245,256]{1,0:T(8,128)S(1)}, u32[]{:S(2)}) copy-start(f32[245,256]{1,0:T(8,128)S(1)} %get-tuple-element.85) | copy-start | bytes 752644
  7.4 7.9 %copy-start.32 = (f32[245,256]{1,0:T(8,128)}, f32[245,256]{1,0:T(8,128)S(1)}, u32[]{:S(2)}) copy-start(f32[245,256]{1,0:T(8,128)S(1)} %get-tuple-element.86) | copy-start | bytes 752644
  7.4 7.9 %copy-start.25 = (f32[246,256]{1,0:T(8,128)}, f32[246,256]{1,0:T(8,128)S(1)}, u32[]{:S(2)}) copy-start(f32[246,256]{1,0:T(8,128)S(1)} %get-tuple-element.87) | copy-start | bytes 755716
  7.4 7.9 %copy-start.33 = (f32[246,256]{1,0:T(8,128)}, f32[246,256]{1,0:T(8,128)S(1)}, u32[]{:S(2)}) copy-start(f32[246,256]{1,0:T(8,128)S(1)} %get-tuple-element.88) | copy-start | bytes 755716
  7.5 7.8 %copy-start.26 = (f32[247,256]{1,0:T(8,128)}, f32[247,256]{1,0:T(8,128)S(1)}, u32[]{:S(2)}) copy-start(f32[247,256]{1,0:T(8,128)S(1)} %get-tuple-element.89) | copy-start | bytes 758788
  7.5 7.8 %copy-start.34 = (f32[247,256]{1,0:T(8,128)}, f32[247,256]{1,0:T(8,128)S(1)}, u32[]{:S(2)}) copy-start(f32[247,256]{1,0:T(8,128)S(1)} %get-tuple-element.90) | copy-start | bytes 758788
  8.0 7.3 %copy-start.27 = (f32[248,256]{1,0:T(8,128)}, f32[248,256]{1,0:T(8,128)S(1)}, u32[]{:S(2)}) copy-start(f32[248,256]{1,0:T(8,128)S(1)} %get-tuple-element.91) | copy-start | bytes 761860
  8.0 7.4 %copy-start.35 = (f32[248,256]{1,0:T(8,128)}, f32[248,256]{1,0:T(8,128)S(1)}, u32[]{:S(2)}) copy-start(f32[248,256]{1,0:T(8,128)S(1)} %get-tuple-element.92) | copy-start | bytes 761860
  10.4 4.9 %copy-start.55 = (f32[256]{0:T(256)}, f32[256]{0:T(256)S(1)}, u32[]{:S(2)}) copy-start(f32[256]{0:T(256)S(1)} %get-tuple-element.160) | copy-start | bytes 3076
  10.4 4.9 %copy-start.58 = (f32[256]{0:T(256)}, f32[256]{0:T(256)S(1)}, u32[]{:S(2)}) copy-start(f32[256]{0:T(256)S(1)} %get-tuple-element.161) | copy-start | bytes 3076
  10.4 4.9 %copy-start.61 = (f32[256]{0:T(256)}, f32[256]{0:T(256)S(1)}, u32[]{:S(2)}) copy-start(f32[256]{0:T(256)S(1)} %get-tuple-element.162) | copy-start | bytes 3076
  10.4 4.9 %copy-start.64 = (f32[256]{0:T(256)}, f32[256]{0:T(256)S(1)}, u32[]{:S(2)}) copy-start(f32[256]{0:T(256)S(1)} %get-tuple-element.163) | copy-start | bytes 3076
  10.5 4.9 %copy-start.66 = (f32[256]{0:T(256)}, f32[256]{0:T(256)S(1)}, u32[]{:S(2)}) copy-start(f32[256]{0:T(256)S(1)} %get-tuple-element.164) | copy-start | bytes 3076
  10.5 4.9 %copy-start.68 = (f32[256]{0:T(256)}, f32[256]{0:T(256)S(1)}, u32[]{:S(2)}) copy-start(f32[256]{0:T(256)S(1)} %get-tuple-element.165) | copy-start | bytes 3076
  11.1 4.3 %copy-start.43 = (f32[256]{0:T(256)}, f32[256]{0:T(256)S(1)}, u32[]{:S(2)}) copy-start(f32[256]{0:T(256)S(1)} %get-tuple-element.145) | copy-start | bytes 3076
  11.1 4.3 %copy-start.45 = (f32[256]{0:T(256)}, f32[256]{0:T(256)S(1)}, u32[]{:S(2)}) copy-start(f32[256]{0:T(256)S(1)} %get-tuple-element.146) | copy-start | bytes 3076
  11.1 4.3 %copy-start.47 = (f32[256]{0:T(256)}, f32[256]{0:T(256)S(1)}, u32[]{:S(2)}) copy-start(f32[256]{0:T(256)S(1)} %get-tuple-element.147) | copy-start | bytes 3076
  11.1 4.3 %copy-start.49 = (f32[256]{0:T(256)}, f32[256]{0:T(256)S(1)}, u32[]{:S(2)}) copy-start(f32[256]{0:T(256)S(1)} %get-tuple-element.148) | copy-start | bytes 3076
  11.2 4.3 %copy-start.51 = (f32[256]{0:T(256)}, f32[256]{0:T(256)S(1)}, u32[]{:S(2)}) copy-start(f32[256]{0:T(256)S(1)} %get-tuple-element.149) | copy-start | bytes 3076
  11.2 4.3 %copy-start.53 = (f32[256]{0:T(256)}, f32[256]{0:T(256)S(1)}, u32[]{:S(2)}) copy-start(f32[256]{0:T(256)S(1)} %get-tuple-element.150) | copy-start | bytes 3076
  15.4 66.6 %copy-start.40 = (f32[256,256]{1,0:T(8,128)}, f32[256,256]{1,0:T(8,128)S(1)}, u32[]{:S(2)}) copy-start(f32[256,256]{1,0:T(8,128)S(1)} %get-tuple-element.46) | copy-start | bytes 786436
  20.6 29.7 %all-to-all-start = ((f32[64,2,256]{2,1,0:T(2,128)}), f32[64,2,256]{2,1,0:T(2,128)}, u32[]{:S(2)}, u32[]{:S(2)}) async-start(f32[64,2,256]{2,1,0:T(2,128)} %broadcast_in_dim.4), calls=%async_computation | async-start | bytes 262144 | tf_op jit(solution)/shard_map/all_to_all | solution.py:37
  52.6 2.8 %copy-start.72 = (f32[1,256]{1,0:T(1,128)}, f32[1,256]{1,0:T(1,128)S(1)}, u32[]{:S(2)}) copy-start(f32[1,256]{1,0:T(1,128)S(1)} %get-tuple-element.45) | copy-start | bytes 3076
  60.5 18.7 %all-to-all-start.1 = ((f32[64,2,256]{2,1,0:T(2,128)}), f32[64,2,256]{2,1,0:T(2,128)}, u32[]{:S(2)}, u32[]{:S(2)}) async-start(f32[64,2,256]{2,1,0:T(2,128)} %broadcast_in_dim.5), calls=%async_computation.1 | async-start | bytes 262144 | tf_op jit(solution)/shard_map/all_to_all | solution.py:37
  82.1 3.1 %copy-start.70 = (f32[1,256]{1,0:T(1,128)}, f32[1,256]{1,0:T(1,128)S(1)}, u32[]{:S(2)}) copy-start(f32[1,256]{1,0:T(1,128)S(1)} %get-tuple-element.140) | copy-start | bytes 3076
  85.4 0.7 copy-start.48
  90.1 1.3 copy-start.41
  99.3 9.0 %collective-permute-start = (bf16[64,8,768]{2,1,0:T(8,128)(2,1)}, bf16[64,8,768]{2,1,0:T(8,128)(2,1)}, u32[]{:S(2)}, u32[]{:S(2)}) collective-permute-start(bf16[64,8,768]{2,1,0:T(8,128)(2,1)} %fusion.3), channel_id=1, source_target_pairs={{0,4},{4,0},{1,5},{5,1},{2,6},{6,2},{3,7},{7,3},{8,12},{12,8},{9,1... | collective-permute-start | bytes 2359304 | tf_op jit(solution)/shard_map/ppermute | solution.py:47
  103.5 13.5 %all-to-all-start.2 = ((bf16[4,256,256]{2,1,0:T(8,128)(2,1)}), bf16[4,256,256]{2,1,0:T(8,128)(2,1)S(1)}, u32[]{:S(2)}, u32[]{:S(2)}) async-start(bf16[4,256,256]{2,1,0:T(8,128)(2,1)} %bitcast.101), calls=%async_computation.2 | async-start | bytes 1048576 | tf_op jit(solution)/shard_map/all_to_all | solution.py:119
  108.3 16.5 %copy-start.2 = (f32[251,256]{1,0:T(8,128)S(1)}, f32[251,256]{1,0:T(8,128)}, u32[]{:S(2)}) copy-start(f32[251,256]{1,0:T(8,128)} %copy-done.1) | copy-start | bytes 771076
  108.3 16.5 %copy-start.63 = (f32[256]{0:T(256)S(1)}, f32[256]{0:T(256)}, u32[]{:S(2)}) copy-start(f32[256]{0:T(256)} %copy-done.61) | copy-start | bytes 3076
  111.0 16.3 %copy-start.5 = (f32[252,256]{1,0:T(8,128)S(1)}, f32[252,256]{1,0:T(8,128)}, u32[]{:S(2)}) copy-start(f32[252,256]{1,0:T(8,128)} %copy-done.4) | copy-start | bytes 774148
  111.0 16.3 %copy-start.7 = (f32[253,256]{1,0:T(8,128)S(1)}, f32[253,256]{1,0:T(8,128)}, u32[]{:S(2)}) copy-start(f32[253,256]{1,0:T(8,128)} %copy-done.6) | copy-start | bytes 777220
  111.0 16.3 %copy-start.57 = (f32[256]{0:T(256)S(1)}, f32[256]{0:T(256)}, u32[]{:S(2)}) copy-start(f32[256]{0:T(256)} %copy-done.55) | copy-start | bytes 3076
  111.0 16.3 %copy-start.60 = (f32[256]{0:T(256)S(1)}, f32[256]{0:T(256)}, u32[]{:S(2)}) copy-start(f32[256]{0:T(256)} %copy-done.58) | copy-start | bytes 3076
  117.0 0.8 copy-start.36
  117.8 77.2 %all-to-all-start.3 = ((bf16[64,8,768]{2,1,0:T(8,128)(2,1)}), bf16[64,8,768]{2,1,0:T(8,128)(2,1)S(1)}, u32[]{:S(2)}, u32[]{:S(2)}) async-start(bf16[64,8,768]{2,1,0:T(8,128)(2,1)} %fusion), calls=%async_computation.3 | async-start | bytes 1572864 | tf_op jit(solution)/shard_map/all_to_all | solution.py:49
  122.4 4.9 %copy-start.9 = (f32[254,256]{1,0:T(8,128)S(1)}, f32[254,256]{1,0:T(8,128)}, u32[]{:S(2)}) copy-start(f32[254,256]{1,0:T(8,128)} %copy-done.8) | copy-start | bytes 780292
  122.4 4.9 %copy-start.11 = (f32[254,256]{1,0:T(8,128)S(1)}, f32[254,256]{1,0:T(8,128)}, u32[]{:S(2)}) copy-start(f32[254,256]{1,0:T(8,128)} %copy-done.10) | copy-start | bytes 780292
  122.4 4.9 %copy-start.13 = (f32[255,256]{1,0:T(8,128)S(1)}, f32[255,256]{1,0:T(8,128)}, u32[]{:S(2)}) copy-start(f32[255,256]{1,0:T(8,128)} %copy-done.12) | copy-start | bytes 783364
  122.4 4.9 %copy-start.15 = (f32[255,256]{1,0:T(8,128)S(1)}, f32[255,256]{1,0:T(8,128)}, u32[]{:S(2)}) copy-start(f32[255,256]{1,0:T(8,128)} %copy-done.14) | copy-start | bytes 783364
  122.5 4.9 %copy-start.17 = (f32[250,256]{1,0:T(8,128)S(1)}, f32[250,256]{1,0:T(8,128)}, u32[]{:S(2)}) copy-start(f32[250,256]{1,0:T(8,128)} %copy-done.16) | copy-start | bytes 768004
  122.5 4.9 %copy-start.19 = (f32[251,256]{1,0:T(8,128)S(1)}, f32[251,256]{1,0:T(8,128)}, u32[]{:S(2)}) copy-start(f32[251,256]{1,0:T(8,128)} %copy-done.18) | copy-start | bytes 771076
  127.4 66.8 %copy-start.37 = (bf16[4,256,256]{2,1,0:T(8,128)(2,1)S(1)}, bf16[4,256,256]{2,1,0:T(8,128)(2,1)}, u32[]{:S(2)}) copy-start(bf16[4,256,256]{2,1,0:T(8,128)(2,1)} %copy-done.36) | copy-start | bytes 1572868
  (14 other events, 9.2 us)
